TPU v7x, 512 devices: a whole 4x8x8 slice. The times are simulated.
512 devices in a mesh: row: 16 (over z, core), col: 32 (over x, y).
Axes of the slice: x: 4, y: 8, z: 8, core: 2. Of those that a mesh axis runs over, the one named last changes fastest.
Arguments:
- panels: float32 [8192, 16384], P('row', 'col'), as said below
Outputs:
- r_rows: float32 [256, 16384], P(None, 'col')
Inputs may be any that keep to these rules, and one draw needn't show every extreme that they name: `panels`: the first 256 columns of W have full column rank.
All inputs are finite; a program needn't handle non-finite values.
Results may differ from a plain program's by a relative error of at most 0.0003.
Values sent between devices are 32-bit elements; how exact they have to be, the bound alone decides.
A program may use at most 64 MiB of HBM per device.

v0:
```python
import jax
import jax.numpy as jnp
from jax import lax
from jax.sharding import PartitionSpec as P

PANEL = 128


def swapped(shard, axis, distance):
    return lax.ppermute(shard, axis, [(i, i ^ 1 << distance) for i in range(lax.axis_size(axis))])


def spread_2(block, axis, source):
    block = jnp.where(lax.axis_index(axis) == source, block, jnp.zeros_like(block))
    return lax.psum(block, axis)


def matmul(left, right):
    return jnp.dot(left, right, precision=lax.Precision.HIGHEST, preferred_element_type=jnp.float32)


def contract_rows(left, right):
    return lax.dot_general(
        left,
        right,
        (((0,), (0,)), ((), ())),
        precision=lax.Precision.HIGHEST,
        preferred_element_type=jnp.float32,
    )


def outer_rows(left, right):
    return lax.dot_general(
        left,
        right,
        (((1,), (1,)), ((), ())),
        precision=lax.Precision.HIGHEST,
        preferred_element_type=jnp.float32,
    )


def factor(columns):
    first_low = jnp.linalg.cholesky(contract_rows(columns, columns))
    basis_one = jax.scipy.linalg.solve_triangular(first_low, columns.T, lower=True)
    second_low = jnp.linalg.cholesky(outer_rows(basis_one, basis_one))
    basis_t = jax.scipy.linalg.solve_triangular(second_low, basis_one, lower=True)
    triangle = matmul(first_low, second_low).T
    return (basis_t, triangle)


def lower_side(level_bit):
    return lax.axis_index("row") >> level_bit & 1 == 0


def stack_pair(mine, other, is_lower):
    return jnp.concatenate(
        [jnp.where(is_lower, mine, other), jnp.where(is_lower, other, mine)], axis=0
    )


def own_half(level_basis, is_lower):
    start = jnp.where(is_lower, 0, PANEL).astype(jnp.int32)
    return lax.dynamic_slice_in_dim(level_basis, start, PANEL, 1)


def spread_back(halves, top_rows, basis_t, working):
    spread = top_rows
    for my_half in reversed(halves):
        spread = contract_rows(my_half, spread)
    return working - contract_rows(basis_t, spread)


def owner_step(working, panels, panel_index):
    depth_count = lax.axis_size("row").bit_length() - 1
    is_owner = lax.axis_index("col") == panel_index
    columns = jnp.where(is_owner, working[:, :PANEL], panels[:, :PANEL])
    basis_t, triangle = factor(columns)
    level_list = []
    for level_bit in range(depth_count):
        other_tri = swapped(triangle, "row", level_bit)
        level_basis, triangle = factor(stack_pair(triangle, other_tri, lower_side(level_bit)))
        level_list.append(level_basis)
    basis_t, level_stack = (
        spread_2(basis_t, "col", panel_index),
        spread_2(jnp.stack(level_list), "col", panel_index),
    )
    top_rows = matmul(basis_t, working)
    halves = []
    for level_bit in range(depth_count):
        other_top = swapped(top_rows, "row", level_bit)
        is_lower = lower_side(level_bit)
        top_rows = matmul(level_stack[level_bit], stack_pair(top_rows, other_top, is_lower))
        halves.append(own_half(level_stack[level_bit], is_lower))
    return (top_rows, spread_back(halves, top_rows, basis_t, working))


def local(panels):
    working = panels
    pieces = []
    for panel_index in range(2):
        top_rows, working = owner_step(working, panels, panel_index)
        pieces.append(top_rows)
    top_block = jnp.concatenate(pieces, axis=0)
    local_width = panels.shape[1]
    col_iota = jnp.arange(local_width, dtype=jnp.int32)
    global_col = (
        col_iota // PANEL * lax.axis_size("col") + lax.axis_index("col")
    ) * PANEL + col_iota % PANEL
    row_iota = jnp.arange(2 * PANEL, dtype=jnp.int32)
    keep_mask = global_col[None, :] >= row_iota[:, None]
    return jnp.where(keep_mask, top_block, jnp.zeros_like(top_block))


def solution(mesh):
    return jax.shard_map(
        local, mesh=mesh, in_specs=(P("row", "col"),), out_specs=P(None, "col"), check_vma=False
    )
```

profile of v0, /device:TPU:1, one launch (start us, length us, event | category | flops | bytes accessed | tf_op | source)
XLA Modules:
  0.0 1003.0 jit_solution(15096186413171939091)
XLA Ops:
  8.3 11.7 %cholesky.314 = f32[128,128]{1,0:T(8,128)S(1)} custom-call(f32[128,128]{1,0:T(8,128)S(1)} %fusion.119), custom_call_target="Cholesky" | custom-call | tf_op jit(solution)/shard_map/jit(cholesky)/cholesky | solution.py:43
  33.0 11.7 %cholesky.325 = f32[128,128]{1,0:T(8,128)S(1)} custom-call(f32[128,128]{1,0:T(8,128)S(1)} %fusion.117), custom_call_target="Cholesky" | custom-call | tf_op jit(solution)/shard_map/jit(cholesky)/cholesky | solution.py:45
  68.3 11.7 %cholesky.336 = f32[128,128]{1,0:T(8,128)S(1)} custom-call(f32[128,128]{1,0:T(8,128)S(1)} %fusion.116), custom_call_target="Cholesky" | custom-call | tf_op jit(solution)/shard_map/jit(cholesky)/cholesky | solution.py:43
  91.9 22.8 %cholesky.347 = f32[128,128]{1,0:T(8,128)S(1)} custom-call(f32[128,128]{1,0:T(8,128)S(1)} %fusion.114), custom_call_target="Cholesky" | custom-call | tf_op jit(solution)/shard_map/jit(cholesky)/cholesky | solution.py:45
  133.6 11.7 %cholesky.358 = f32[128,128]{1,0:T(8,128)S(1)} custom-call(f32[128,128]{1,0:T(8,128)S(1)} %fusion.112), custom_call_target="Cholesky" | custom-call | tf_op jit(solution)/shard_map/jit(cholesky)/cholesky | solution.py:43
  157.2 11.7 %cholesky.369 = f32[128,128]{1,0:T(8,128)S(1)} custom-call(f32[128,128]{1,0:T(8,128)S(1)} %fusion.110), custom_call_target="Cholesky" | custom-call | tf_op jit(solution)/shard_map/jit(cholesky)/cholesky | solution.py:45
  190.7 11.7 %cholesky.380 = f32[128,128]{1,0:T(8,128)S(1)} custom-call(f32[128,128]{1,0:T(8,128)S(1)} %fusion.108), custom_call_target="Cholesky" | custom-call | tf_op jit(solution)/shard_map/jit(cholesky)/cholesky | solution.py:43
  214.3 11.7 %cholesky.391 = f32[128,128]{1,0:T(8,128)S(1)} custom-call(f32[128,128]{1,0:T(8,128)S(1)} %fusion.106), custom_call_target="Cholesky" | custom-call | tf_op jit(solution)/shard_map/jit(cholesky)/cholesky | solution.py:45
  248.5 11.7 %cholesky.402 = f32[128,128]{1,0:T(8,128)S(1)} custom-call(f32[128,128]{1,0:T(8,128)S(1)} %fusion.104), custom_call_target="Cholesky" | custom-call | tf_op jit(solution)/shard_map/jit(cholesky)/cholesky | solution.py:43
  272.1 11.7 %cholesky.413 = f32[128,128]{1,0:T(8,128)S(1)} custom-call(f32[128,128]{1,0:T(8,128)S(1)} %fusion.102), custom_call_target="Cholesky" | custom-call | tf_op jit(solution)/shard_map/jit(cholesky)/cholesky | solution.py:45
  296.6 156.7 %all-reduce.7.cloned.1.call-done = (f32[128,512]{1,0:T(8,128)}, f32[4,128,256]{2,1,0:T(8,128)}) async-done(((f32[128,512]{1,0:T(8,128)}, f32[4,128,256]{2,1,0:T(8,128)}), (f32[128,512]{1,0:T(8,128)}, f32[4,128,256]{2,1,0:T(8,128)})) %all-reduce.7.cloned.1.call-update) | async-done | bytes 786448 | tf_op jit(solution)/shard_map/psum | solution.py:15
  498.6 11.5 %collective-permute-done.7 = f32[128,512]{1,0:T(8,128)S(1)} collective-permute-done((f32[128,512]{1,0:T(8,128)S(1)}, f32[128,512]{1,0:T(8,128)S(1)}, u32[]{:S(2)}, u32[]{:S(2)}) %collective-permute-start.7) | collective-permute-done | bytes 262176 | tf_op jit(solution)/shard_map/ppermute | solution.py:10
  514.7 11.7 %cholesky.424 = f32[128,128]{1,0:T(8,128)S(1)} custom-call(f32[128,128]{1,0:T(8,128)S(1)} %fusion.91), custom_call_target="Cholesky" | custom-call | tf_op jit(solution)/shard_map/jit(cholesky)/cholesky | solution.py:43
  538.5 11.9 %cholesky.435 = f32[128,128]{1,0:T(8,128)S(1)} custom-call(f32[128,128]{1,0:T(8,128)S(1)} %fusion.89), custom_call_target="Cholesky" | custom-call | tf_op jit(solution)/shard_map/jit(cholesky)/cholesky | solution.py:45
  568.2 11.7 %cholesky.446 = f32[128,128]{1,0:T(8,128)S(1)} custom-call(f32[128,128]{1,0:T(8,128)S(1)} %fusion.88), custom_call_target="Cholesky" | custom-call | tf_op jit(solution)/shard_map/jit(cholesky)/cholesky | solution.py:43
  591.8 12.1 %cholesky.457 = f32[128,128]{1,0:T(8,128)S(1)} custom-call(f32[128,128]{1,0:T(8,128)S(1)} %fusion.86), custom_call_target="Cholesky" | custom-call | tf_op jit(solution)/shard_map/jit(cholesky)/cholesky | solution.py:45
  622.8 11.7 %cholesky.468 = f32[128,128]{1,0:T(8,128)S(1)} custom-call(f32[128,128]{1,0:T(8,128)S(1)} %fusion.84), custom_call_target="Cholesky" | custom-call | tf_op jit(solution)/shard_map/jit(cholesky)/cholesky | solution.py:43
  646.4 11.7 %cholesky.479 = f32[128,128]{1,0:T(8,128)S(1)} custom-call(f32[128,128]{1,0:T(8,128)S(1)} %fusion.82), custom_call_target="Cholesky" | custom-call | tf_op jit(solution)/shard_map/jit(cholesky)/cholesky | solution.py:45
  679.5 11.7 %cholesky.490 = f32[128,128]{1,0:T(8,128)S(1)} custom-call(f32[128,128]{1,0:T(8,128)S(1)} %fusion.80), custom_call_target="Cholesky" | custom-call | tf_op jit(solution)/shard_map/jit(cholesky)/cholesky | solution.py:43
  703.1 11.7 %cholesky.501 = f32[128,128]{1,0:T(8,128)S(1)} custom-call(f32[128,128]{1,0:T(8,128)S(1)} %fusion.78), custom_call_target="Cholesky" | custom-call | tf_op jit(solution)/shard_map/jit(cholesky)/cholesky | solution.py:45
  738.4 11.7 %cholesky.512 = f32[128,128]{1,0:T(8,128)S(1)} custom-call(f32[128,128]{1,0:T(8,128)S(1)} %fusion.76), custom_call_target="Cholesky" | custom-call | tf_op jit(solution)/shard_map/jit(cholesky)/cholesky | solution.py:43
  761.9 11.7 %cholesky.523 = f32[128,128]{1,0:T(8,128)S(1)} custom-call(f32[128,128]{1,0:T(8,128)S(1)} %fusion.74), custom_call_target="Cholesky" | custom-call | tf_op jit(solution)/shard_map/jit(cholesky)/cholesky | solution.py:45
  786.2 151.2 %all-reduce.5.cloned.1.call-done = (f32[128,512]{1,0:T(8,128)}, f32[4,128,256]{2,1,0:T(8,128)}) async-done(((f32[128,512]{1,0:T(8,128)}, f32[4,128,256]{2,1,0:T(8,128)}), (f32[128,512]{1,0:T(8,128)}, f32[4,128,256]{2,1,0:T(8,128)})) %all-reduce.5.cloned.1.call-update) | async-done | bytes 786448 | tf_op jit(solution)/shard_map/psum | solution.py:15
  982.8 11.6 %collective-permute-done.15 = f32[128,512]{1,0:T(8,128)S(1)} collective-permute-done((f32[128,512]{1,0:T(8,128)S(1)}, f32[128,512]{1,0:T(8,128)S(1)}, u32[]{:S(2)}, u32[]{:S(2)}) %collective-permute-start.15) | collective-permute-done | bytes 262176 | tf_op jit(solution)/shard_map/ppermute | solution.py:10
  (246 shorter events, 410.9 us)
Async XLA Ops:
  6.5 446.7 %all-reduce.7.cloned.1.call-start = ((), (), s32[]{:S(2)}) async-start(), calls=%async_computation.1 | async-start | bytes 1572864 | tf_op jit(solution)/shard_map/psum | solution.py:15
  47.1 20.7 %collective-permute-start = (f32[128,128]{1,0:T(8,128)S(1)}, f32[128,128]{1,0:T(8,128)S(1)}, u32[]{:S(2)}, u32[]{:S(2)}) collective-permute-start(f32[128,128]{1,0:T(8,128)S(1)} %fusion.141), channel_id=1, source_target_pairs={{0,32},{32,0},{64,96},{96,64},{128,160},{160,128},{192,224},{224,1... | collective-permute-start | bytes 196616 | tf_op jit(solution)/shard_map/ppermute | solution.py:10
  127.6 5.5 collective-permute-start.1
  182.2 7.9 collective-permute-start.2
  239.1 8.9 collective-permute-start.3
  295.3 157.9 %copy-start = (f32[512,512]{1,0:T(8,128)S(1)}, f32[512,512]{1,0:T(8,128)}, u32[]{:S(2)}) copy-start(f32[512,512]{1,0:T(8,128)} %param.6) | copy-start | bytes 3145732
  296.5 640.9 %all-reduce.5.cloned.1.call-start = ((), (), s32[]{:S(2)}) async-start(), calls=%async_computation | async-start | bytes 1572864 | tf_op jit(solution)/shard_map/psum | solution.py:15
  454.9 8.7 copy-start.1
  454.9 8.6 collective-permute-start.4
  464.0 9.4 collective-permute-start.5
  473.9 15.7 %collective-permute-start.6 = (f32[128,512]{1,0:T(8,128)S(1)}, f32[128,512]{1,0:T(8,128)S(1)}, u32[]{:S(2)}, u32[]{:S(2)}) collective-permute-start(f32[128,512]{1,0:T(8,128)S(1)} %fusion.4), channel_id=1, source_target_pairs={{0,128},{32,160},{64,192},{96,224},{128,0},{160,32},{192,64},{224,... | collective-permute-start | bytes 786440 | tf_op jit(solution)/shard_map/ppermute | solution.py:10
  490.0 20.1 %collective-permute-start.7 = (f32[128,512]{1,0:T(8,128)S(1)}, f32[128,512]{1,0:T(8,128)S(1)}, u32[]{:S(2)}, u32[]{:S(2)}) collective-permute-start(f32[128,512]{1,0:T(8,128)S(1)} %fusion.8), channel_id=1, source_target_pairs={{0,256},{32,288},{64,320},{96,352},{128,384},{160,416},{192,448},{... | collective-permute-start | bytes 786440 | tf_op jit(solution)/shard_map/ppermute | solution.py:10
  512.0 1.0 copy-start.2
  553.5 14.2 %collective-permute-start.8 = (f32[128,128]{1,0:T(8,128)S(1)}, f32[128,128]{1,0:T(8,128)S(1)}, u32[]{:S(2)}, u32[]{:S(2)}) collective-permute-start(f32[128,128]{1,0:T(8,128)S(1)} %fusion.146), channel_id=1, source_target_pairs={{0,32},{32,0},{64,96},{96,64},{128,160},{160,128},{192,224},{224,1... | collective-permute-start | bytes 196616 | tf_op jit(solution)/shard_map/ppermute | solution.py:10
  616.8 5.5 collective-permute-start.9
  671.2 7.8 collective-permute-start.10
  727.9 9.9 collective-permute-start.11
  939.1 8.7 copy-start.3
  939.1 8.6 collective-permute-start.12
  948.2 9.4 collective-permute-start.13
  958.1 15.7 %collective-permute-start.14 = (f32[128,512]{1,0:T(8,128)S(1)}, f32[128,512]{1,0:T(8,128)S(1)}, u32[]{:S(2)}, u32[]{:S(2)}) collective-permute-start(f32[128,512]{1,0:T(8,128)S(1)} %fusion.20), channel_id=1, source_target_pairs={{0,128},{32,160},{64,192},{96,224},{128,0},{160,32},{192,64},{224,... | collective-permute-start | bytes 786440 | tf_op jit(solution)/shard_map/ppermute | solution.py:10
  974.2 20.1 %collective-permute-start.15 = (f32[128,512]{1,0:T(8,128)S(1)}, f32[128,512]{1,0:T(8,128)S(1)}, u32[]{:S(2)}, u32[]{:S(2)}) collective-permute-start(f32[128,512]{1,0:T(8,128)S(1)} %fusion.24), channel_id=1, source_target_pairs={{0,256},{32,288},{64,320},{96,352},{128,384},{160,416},{192,448},{... | collective-permute-start | bytes 786440 | tf_op jit(solution)/shard_map/ppermute | solution.py:10
Sparse Core Ops, SparseCore 0:
  296.6 156.5 all-reduce.6
  786.3 151.0 all-reduce.4
where the time goes:
time: 1010 us; the launch traced here: 1000 us
  other arithmetic  474 us (47%)
  waiting for transfers between devices  395 us (39%)
  starting transfers between devices  76.4 us (8%)
  matrix products  39.8 us (4%)
  between operations  15.2 us (2%)
    psum x2, waiting for transfers between devices, spread_2(): return lax.psum(block, axis)  308 us
    another operation x30, other arithmetic, factor(): second_low = jnp.linalg.cholesky(outer_rows(basis_one, basis_one))  136 us
    another operation x30, other arithmetic, factor(): first_low = jnp.linalg.cholesky(contract_rows(columns, columns))  124 us
    another operation x20, other arithmetic, factor(): jax.scipy.linalg.solve_triangular(second_low, basis_one, lower=True)  106 us
    another operation x20, other arithmetic, factor(): jax.scipy.linalg.solve_triangular(first_low, columns.T, lower=True)  105 us
    ppermute x16, waiting for transfers between devices, swapped(): lax.ppermute(shard, axis, [(i, i ^ 1 << distance) for i in range(lax.axis...  87 us
    ppermute x16, starting transfers between devices, swapped(): lax.ppermute(shard, axis, [(i, i ^ 1 << distance) for i in range(lax.axis...  76.3 us
  transfers between devices with their start and end apart: 18, of which 16 were waited for; matrix products, arithmetic and copies ran while one was open for 2% of the time, Pallas kernels for 0%

commit v1 on v0

--- a/solution.py
+++ b/solution.py
@@ -12,7 +12,7 @@
 
 def spread_2(block, axis, source):
     block = jnp.where(lax.axis_index(axis) == source, block, jnp.zeros_like(block))
-    return lax.psum(block, axis)
+    return jnp.sum(jax.lax.all_gather(block, axis), axis=0)
 
 
 def matmul(left, right):

time: 1010 us -> 979 us (0.969)
  waiting for transfers between devices: 395 us -> 348 us
  other arithmetic: 474 us -> 495 us
    psum x2 -> x0, waiting for transfers between devices: 308 us -> none  [spread_2(): return lax.psum(block, axis)]
    all_gather x0 -> x4, waiting for transfers between devices: none -> 264 us  [spread_2(): return jnp.sum(jax.lax.all_gather(block, axis), axis=0)]
    reduce_sum x0 -> x4, other arithmetic: none -> 22.4 us  [spread_2(): return jnp.sum(jax.lax.all_gather(block, axis), axis=0)]
    another operation x30, other arithmetic: 136 us -> 125 us  [factor(): second_low = jnp.linalg.cholesky(outer_rows(basis_one, basis_one))]
  transfers between devices with their start and end apart: 18 -> 20, of which waited for: 16 -> 18; matrix products, arithmetic and copies ran while one was open for 2% -> 43% of each run, Pallas kernels for 0% -> 0%
where the time goes in v1:
time: 979 us; the launch traced here: 969 us
  other arithmetic  495 us (51%)
  waiting for transfers between devices  348 us (36%)
  starting transfers between devices  71.6 us (7%)
  matrix products  37.9 us (4%)
  between operations  14.9 us (2%)
    all_gather x4, waiting for transfers between devices, spread_2(): return jnp.sum(jax.lax.all_gather(block, axis), axis=0)  264 us
    another operation x30, other arithmetic, factor(): second_low = jnp.linalg.cholesky(outer_rows(basis_one, basis_one))  125 us
    another operation x30, other arithmetic, factor(): first_low = jnp.linalg.cholesky(contract_rows(columns, columns))  124 us
    another operation x20, other arithmetic, factor(): jax.scipy.linalg.solve_triangular(second_low, basis_one, lower=True)  116 us
    another operation x20, other arithmetic, factor(): jax.scipy.linalg.solve_triangular(first_low, columns.T, lower=True)  105 us
    ppermute x16, waiting for transfers between devices, swapped(): lax.ppermute(shard, axis, [(i, i ^ 1 << distance) for i in range(lax.axis...  83.4 us
    ppermute x16, starting transfers between devices, swapped(): lax.ppermute(shard, axis, [(i, i ^ 1 << distance) for i in range(lax.axis...  71.5 us
    reduce_sum x4, other arithmetic, spread_2(): return jnp.sum(jax.lax.all_gather(block, axis), axis=0)  22.4 us
  transfers between devices with their start and end apart: 20, of which 18 were waited for; matrix products, arithmetic and copies ran while one was open for 43% of the time, Pallas kernels for 0%

profile of v1, /device:TPU:1, one launch (start us, length us, event | category | flops | bytes accessed | tf_op | source)
XLA Modules:
  0.0 969.5 jit_solution(16762615499997640943)
XLA Ops:
  8.4 11.7 %cholesky.314 = f32[128,128]{1,0:T(8,128)S(1)} custom-call(f32[128,128]{1,0:T(8,128)S(1)} %fusion.119), custom_call_target="Cholesky" | custom-call | tf_op jit(solution)/shard_map/jit(cholesky)/cholesky | solution.py:43
  33.1 11.7 %cholesky.325 = f32[128,128]{1,0:T(8,128)S(1)} custom-call(f32[128,128]{1,0:T(8,128)S(1)} %fusion.117), custom_call_target="Cholesky" | custom-call | tf_op jit(solution)/shard_map/jit(cholesky)/cholesky | solution.py:45
  69.3 11.7 %cholesky.336 = f32[128,128]{1,0:T(8,128)S(1)} custom-call(f32[128,128]{1,0:T(8,128)S(1)} %fusion.116), custom_call_target="Cholesky" | custom-call | tf_op jit(solution)/shard_map/jit(cholesky)/cholesky | solution.py:43
  92.9 11.7 %cholesky.347 = f32[128,128]{1,0:T(8,128)S(1)} custom-call(f32[128,128]{1,0:T(8,128)S(1)} %fusion.114), custom_call_target="Cholesky" | custom-call | tf_op jit(solution)/shard_map/jit(cholesky)/cholesky | solution.py:45
  106.1 19.3 %custom-call.28 = f32[1,128,128]{1,2,0:T(8,128)S(1)} custom-call(f32[1,128,128]{2,1,0:T(8,128)S(1)} %select_bitcast_fusion.13), custom_call_target="InvertDiagBlocksLowerTriangular" | custom-call | tf_op jit(solution)/shard_map/jit(_solve_triangular)/triangular_solve | solution.py:46
  132.9 11.7 %cholesky.358 = f32[128,128]{1,0:T(8,128)S(1)} custom-call(f32[128,128]{1,0:T(8,128)S(1)} %fusion.112), custom_call_target="Cholesky" | custom-call | tf_op jit(solution)/shard_map/jit(cholesky)/cholesky | solution.py:43
  156.5 11.7 %cholesky.369 = f32[128,128]{1,0:T(8,128)S(1)} custom-call(f32[128,128]{1,0:T(8,128)S(1)} %fusion.110), custom_call_target="Cholesky" | custom-call | tf_op jit(solution)/shard_map/jit(cholesky)/cholesky | solution.py:45
  189.5 11.7 %cholesky.380 = f32[128,128]{1,0:T(8,128)S(1)} custom-call(f32[128,128]{1,0:T(8,128)S(1)} %fusion.108), custom_call_target="Cholesky" | custom-call | tf_op jit(solution)/shard_map/jit(cholesky)/cholesky | solution.py:43
  213.1 11.7 %cholesky.391 = f32[128,128]{1,0:T(8,128)S(1)} custom-call(f32[128,128]{1,0:T(8,128)S(1)} %fusion.106), custom_call_target="Cholesky" | custom-call | tf_op jit(solution)/shard_map/jit(cholesky)/cholesky | solution.py:45
  247.3 11.7 %cholesky.402 = f32[128,128]{1,0:T(8,128)S(1)} custom-call(f32[128,128]{1,0:T(8,128)S(1)} %fusion.104), custom_call_target="Cholesky" | custom-call | tf_op jit(solution)/shard_map/jit(cholesky)/cholesky | solution.py:43
  270.9 11.7 %cholesky.413 = f32[128,128]{1,0:T(8,128)S(1)} custom-call(f32[128,128]{1,0:T(8,128)S(1)} %fusion.102), custom_call_target="Cholesky" | custom-call | tf_op jit(solution)/shard_map/jit(cholesky)/cholesky | solution.py:45
  306.3 134.4 %all-gather.7.cloned.1.call-done = f32[32,4,128,256]{3,2,1,0:T(8,128)} async-done(((f32[1,4,128,256]{3,2,1,0:T(8,128)}), f32[32,4,128,256]{3,2,1,0:T(8,128)}) %all-gather.7.cloned.1.call-update) | async-done | bytes 16777232 | tf_op jit(solution)/shard_map/all_gather | solution.py:15
  497.2 11.7 %cholesky.424 = f32[128,128]{1,0:T(8,128)S(1)} custom-call(f32[128,128]{1,0:T(8,128)S(1)} %fusion.91), custom_call_target="Cholesky" | custom-call | tf_op jit(solution)/shard_map/jit(cholesky)/cholesky | solution.py:43
  521.0 11.9 %cholesky.435 = f32[128,128]{1,0:T(8,128)S(1)} custom-call(f32[128,128]{1,0:T(8,128)S(1)} %fusion.89), custom_call_target="Cholesky" | custom-call | tf_op jit(solution)/shard_map/jit(cholesky)/cholesky | solution.py:45
  551.6 11.7 %cholesky.446 = f32[128,128]{1,0:T(8,128)S(1)} custom-call(f32[128,128]{1,0:T(8,128)S(1)} %fusion.88), custom_call_target="Cholesky" | custom-call | tf_op jit(solution)/shard_map/jit(cholesky)/cholesky | solution.py:43
  575.2 11.7 %cholesky.457 = f32[128,128]{1,0:T(8,128)S(1)} custom-call(f32[128,128]{1,0:T(8,128)S(1)} %fusion.86), custom_call_target="Cholesky" | custom-call | tf_op jit(solution)/shard_map/jit(cholesky)/cholesky | solution.py:45
  606.2 11.7 %cholesky.468 = f32[128,128]{1,0:T(8,128)S(1)} custom-call(f32[128,128]{1,0:T(8,128)S(1)} %fusion.84), custom_call_target="Cholesky" | custom-call | tf_op jit(solution)/shard_map/jit(cholesky)/cholesky | solution.py:43
  629.7 11.7 %cholesky.479 = f32[128,128]{1,0:T(8,128)S(1)} custom-call(f32[128,128]{1,0:T(8,128)S(1)} %fusion.82), custom_call_target="Cholesky" | custom-call | tf_op jit(solution)/shard_map/jit(cholesky)/cholesky | solution.py:45
  661.6 11.7 %cholesky.490 = f32[128,128]{1,0:T(8,128)S(1)} custom-call(f32[128,128]{1,0:T(8,128)S(1)} %fusion.80), custom_call_target="Cholesky" | custom-call | tf_op jit(solution)/shard_map/jit(cholesky)/cholesky | solution.py:43
  685.2 11.7 %cholesky.501 = f32[128,128]{1,0:T(8,128)S(1)} custom-call(f32[128,128]{1,0:T(8,128)S(1)} %fusion.78), custom_call_target="Cholesky" | custom-call | tf_op jit(solution)/shard_map/jit(cholesky)/cholesky | solution.py:45
  719.5 11.7 %cholesky.512 = f32[128,128]{1,0:T(8,128)S(1)} custom-call(f32[128,128]{1,0:T(8,128)S(1)} %fusion.76), custom_call_target="Cholesky" | custom-call | tf_op jit(solution)/shard_map/jit(cholesky)/cholesky | solution.py:43
  743.0 11.7 %cholesky.523 = f32[128,128]{1,0:T(8,128)S(1)} custom-call(f32[128,128]{1,0:T(8,128)S(1)} %fusion.74), custom_call_target="Cholesky" | custom-call | tf_op jit(solution)/shard_map/jit(cholesky)/cholesky | solution.py:45
  778.7 130.0 %all-gather.9.cloned.1.call-done = f32[32,4,128,256]{3,2,1,0:T(8,128)} async-done(((f32[1,4,128,256]{3,2,1,0:T(8,128)}), f32[32,4,128,256]{3,2,1,0:T(8,128)}) %all-gather.9.cloned.1.call-update) | async-done | bytes 16777232 | tf_op jit(solution)/shard_map/all_gather | solution.py:15
  949.6 11.6 %collective-permute-done.15 = f32[128,512]{1,0:T(8,128)S(1)} collective-permute-done((f32[128,512]{1,0:T(8,128)S(1)}, f32[128,512]{1,0:T(8,128)S(1)}, u32[]{:S(2)}, u32[]{:S(2)}) %collective-permute-start.15) | collective-permute-done | bytes 262176 | tf_op jit(solution)/shard_map/ppermute | solution.py:10
  (250 shorter events, 424.9 us)
Async XLA Ops:
  6.5 293.1 %copy-start = (f32[512,512]{1,0:T(8,128)S(1)}, f32[512,512]{1,0:T(8,128)}, u32[]{:S(2)}) copy-start(f32[512,512]{1,0:T(8,128)} %param.6) | copy-start | bytes 3145732
  6.5 288.9 %all-gather.11.cloned.1.call-start = ((), (), s32[]{:S(2)}) async-start(), calls=%async_computation.2 | async-start | bytes 8650752 | tf_op jit(solution)/shard_map/all_gather | solution.py:15
  57.5 383.2 %all-gather.7.cloned.1.call-start = ((), (), s32[]{:S(2)}) async-start(), calls=%async_computation | async-start | bytes 17301504 | tf_op jit(solution)/shard_map/all_gather | solution.py:15
  59.2 9.6 collective-permute-start
  127.0 5.4 collective-permute-start.1
  181.5 7.5 collective-permute-start.2
  237.9 8.9 collective-permute-start.3
  295.3 472.0 %all-gather.13.cloned.1.call-start = ((), (), s32[]{:S(2)}) async-start(), calls=%async_computation.3 | async-start | bytes 8650752 | tf_op jit(solution)/shard_map/all_gather | solution.py:15
  300.4 5.8 collective-permute-start.4
  448.1 8.4 collective-permute-start.5
  456.9 15.7 %collective-permute-start.6 = (f32[128,512]{1,0:T(8,128)S(1)}, f32[128,512]{1,0:T(8,128)S(1)}, u32[]{:S(2)}, u32[]{:S(2)}) collective-permute-start(f32[128,512]{1,0:T(8,128)S(1)} %fusion.4), channel_id=1, source_target_pairs={{0,128},{32,160},{64,192},{96,224},{128,0},{160,32},{192,64},{224,... | collective-permute-start | bytes 786440 | tf_op jit(solution)/shard_map/ppermute | solution.py:10
  473.0 20.2 %collective-permute-start.7 = (f32[128,512]{1,0:T(8,128)S(1)}, f32[128,512]{1,0:T(8,128)S(1)}, u32[]{:S(2)}, u32[]{:S(2)}) collective-permute-start(f32[128,512]{1,0:T(8,128)S(1)} %fusion.8), channel_id=1, source_target_pairs={{0,256},{32,288},{64,320},{96,352},{128,384},{160,416},{192,448},{... | collective-permute-start | bytes 786440 | tf_op jit(solution)/shard_map/ppermute | solution.py:10
  545.3 363.3 %all-gather.9.cloned.1.call-start = ((), (), s32[]{:S(2)}) async-start(), calls=%async_computation.1 | async-start | bytes 17301504 | tf_op jit(solution)/shard_map/all_gather | solution.py:15
  547.0 4.1 collective-permute-start.8
  600.2 5.4 collective-permute-start.9
  654.5 6.6 collective-permute-start.10
  710.0 8.9 collective-permute-start.11
  772.3 6.3 collective-permute-start.12
  916.1 8.4 collective-permute-start.13
  924.9 15.6 %collective-permute-start.14 = (f32[128,512]{1,0:T(8,128)S(1)}, f32[128,512]{1,0:T(8,128)S(1)}, u32[]{:S(2)}, u32[]{:S(2)}) collective-permute-start(f32[128,512]{1,0:T(8,128)S(1)} %fusion.20), channel_id=1, source_target_pairs={{0,128},{32,160},{64,192},{96,224},{128,0},{160,32},{192,64},{224,... | collective-permute-start | bytes 786440 | tf_op jit(solution)/shard_map/ppermute | solution.py:10
  941.0 20.1 %collective-permute-start.15 = (f32[128,512]{1,0:T(8,128)S(1)}, f32[128,512]{1,0:T(8,128)S(1)}, u32[]{:S(2)}, u32[]{:S(2)}) collective-permute-start(f32[128,512]{1,0:T(8,128)S(1)} %fusion.24), channel_id=1, source_target_pairs={{0,256},{32,288},{64,320},{96,352},{128,384},{160,416},{192,448},{... | collective-permute-start | bytes 786440 | tf_op jit(solution)/shard_map/ppermute | solution.py:10
Sparse Core Ops, SparseCore 0:
  57.6 108.1 all-gather.10
  295.5 145.2 all-gather.6
  545.5 97.6 all-gather.12
  767.4 141.2 all-gather.8
